TPU v7x, 32 devices: a whole 2x2x4 slice. The times are simulated.
32 devices in a mesh: grp: 2 (over y), slab: 16 (over z, x, core).
Axes of the slice: x: 2, y: 2, z: 4, core: 2. Of those that a mesh axis runs over, the one named last changes fastest.
Arguments:
- velocity: float32 [16, 128, 512], P('grp', 'slab'), may hold values from -6 to 6
- rate: float32 [16, 128, 512], P('grp', 'slab'), may hold values from 0.02 to 0.16
- forcing: float32 [16, 128, 512], P('grp', 'slab'), may hold values from -3 to 3
- anchor_line: int32 [512], P(('grp', 'slab')), may hold values from 0 to 63
- anchor_z: int32 [512], P(('grp', 'slab')), may hold values from 0 to 384
- assign: int32 [512, 1], P(('grp', 'slab')), may hold values from 0 to 15; in each aligned block of 16 rows (0 to 15, 16 to 31, ...) at most 2 rows name the same one
- spectral: float32 [2048, 64], replicated, may hold values from -0.75 to 0.75
- dense: float32 [68, 64], replicated, may hold values from -4 to 4
- momentum: float32 [2048, 64], P(('grp', 'slab')), may hold values from -0.3125 to 0.3125
Outputs:
- field_out: float32 [16, 128, 512], P('grp', 'slab')
- trainer_loss: float32 [2, 16], P('grp', 'slab')
- spectral_new: float32 [2048, 64], replicated
- dense_new: float32 [68, 64], replicated
- momentum_new: float32 [2048, 64], P(('grp', 'slab'))
Inputs may be any that keep to these rules, and one draw needn't show every extreme that they name: `assign`: within the 16 lines of one device no trainer is named more than 2 times, and in some device's lines one trainer is named exactly 2 times.
All inputs are finite; a program needn't handle non-finite values.
Results may differ from a plain program's by a relative error of at most 0.0001.
Values sent between devices are 32-bit elements; how exact they have to be, the bound alone decides.
No kernel may reach another device: no remote copies, remote signals or barrier semaphores. Data moves between devices by JAX's collectives and lax.ppermute only.
A program may use at most 64 MiB of HBM per device.

v0:
```python
import jax
import jax.numpy as jnp
from jax import lax
from jax.sharding import PartitionSpec as P

STEPS = 2
SUB = 128
MODES = 16
decay_rate = 0.9
learn_rate = 0.5
dense_rate = 3.0


def extended(cells, sides, width):
    for axis, dim in sides:
        count = lax.axis_size(axis)
        ends = count - 1
        head = lax.slice_in_dim(cells, 0, width, axis=dim)
        tail = lax.slice_in_dim(cells, cells.shape[dim] - width, cells.shape[dim], axis=dim)
        cells = jnp.concatenate(
            [
                lax.ppermute(tail, axis, [(i, (i + 1) % count) for i in range(ends)]),
                cells,
                lax.ppermute(head, axis, [((i + 1) % count, i) for i in range(ends)]),
            ],
            axis=dim,
        )
    return cells


def tables():
    counts = jnp.arange(SUB, dtype=jnp.int32)
    waves = jnp.arange(MODES, dtype=jnp.int32)
    phase = counts[:, None] * waves[None, :] % SUB
    angle = phase.astype(jnp.float32) * (2.0 * jnp.pi / SUB)
    weight_k = jnp.where(waves == 0, 1.0, 2.0).astype(jnp.float32) / SUB
    return (jnp.cos(angle), jnp.sin(angle), weight_k)


def line_errors(spectral, dense, inputs, targets, valid):
    highest = lax.Precision.HIGHEST
    width = dense.shape[1]
    mixing = dense[:width]
    lift_gain, lift_bias, layer_bias, projection = (
        dense[width],
        dense[width + 1],
        dense[width + 2],
        dense[width + 3],
    )
    cosine, sine, weight_k = tables()
    hidden = inputs[:, None, :] * lift_gain[None, :, None] + lift_bias[None, :, None]
    real_in = jnp.einsum("bws,sk->bwk", hidden, cosine, precision=highest)
    imag_in = -jnp.einsum("bws,sk->bwk", hidden, sine, precision=highest)
    blocks = spectral.reshape(2, MODES, width, width)
    w_real, w_imag = (blocks[0], blocks[1])
    real_out = jnp.einsum("bwk,kwv->bvk", real_in, w_real, precision=highest) - jnp.einsum(
        "bwk,kwv->bvk", imag_in, w_imag, precision=highest
    )
    imag_out = jnp.einsum("bwk,kwv->bvk", real_in, w_imag, precision=highest) + jnp.einsum(
        "bwk,kwv->bvk", imag_in, w_real, precision=highest
    )
    spatial = jnp.einsum(
        "bvk,sk->bvs", real_out * weight_k, cosine, precision=highest
    ) - jnp.einsum("bvk,sk->bvs", imag_out * weight_k, sine, precision=highest)
    before = (
        spatial
        + jnp.einsum("bws,wv->bvs", hidden, mixing, precision=highest)
        + layer_bias[None, :, None]
    )
    after = jax.nn.gelu(before)
    output = jnp.einsum("bvs,v->bs", after, projection, precision=highest)
    return jnp.sum((output - targets) ** 2, axis=1) * valid


def gradients_of(spectral, dense, inputs, targets, valid, scale):

    def loss_fn(spec, dens):
        errors = line_errors(spec, dens, inputs, targets, valid)
        return (jnp.sum(errors) * scale, errors)

    value, pullback, errors = jax.vjp(loss_fn, spectral, dense, has_aux=True)
    grad_spec, grad_dense = pullback(jnp.ones((), jnp.float32))
    return (grad_spec, grad_dense, errors)


def local(velocity, rate, forcing, anchor_line, anchor_z, assign, spectral, dense, momentum):
    field_now = velocity
    previous = velocity
    change = velocity
    for number in range(STEPS):
        previous = field_now
        padded = extended(field_now, (("grp", 0), ("slab", 1)), 1)
        beside = padded[2:, 1:-1] + padded[:-2, 1:-1] + padded[1:-1, 2:] + padded[1:-1, :-2]
        beside = beside + jnp.roll(field_now, 1, 2) + jnp.roll(field_now, -1, 2)
        change = rate * (beside - 6.0 * field_now) + forcing
        field_now = field_now + change
    cells_x, cells_y, cells_z = velocity.shape
    line_count = anchor_line.shape[0]
    windows = jax.vmap(lambda row, start: lax.dynamic_slice_in_dim(row, start, SUB))
    inputs = windows(
        jnp.take(previous.reshape(cells_x * cells_y, cells_z), anchor_line, axis=0), anchor_z
    )
    targets = windows(
        jnp.take(change.reshape(cells_x * cells_y, cells_z), anchor_line, axis=0), anchor_z
    )
    n_slab = lax.axis_size("slab")
    devices = lax.axis_size("grp") * n_slab
    scale = 1.0 / (devices * line_count * SUB)
    dest = assign[:, 0]
    onehot = (dest[:, None] == jnp.arange(n_slab, dtype=jnp.int32)[None, :]).astype(jnp.int32)
    grad_spec, grad_dense, errors = gradients_of(
        spectral, dense, inputs, targets, jnp.ones((line_count,), jnp.float32), scale
    )
    partial_loss = jnp.dot(errors, onehot.astype(jnp.float32), precision=lax.Precision.HIGHEST) / (
        line_count * SUB
    )
    trainer_loss = lax.psum_scatter(partial_loss, "slab", scatter_dimension=0, tiled=True).reshape(
        1, 1
    )
    grad_rows = lax.psum_scatter(grad_spec, ("grp", "slab"), scatter_dimension=0, tiled=True)
    grad_dense = lax.psum(grad_dense, ("grp", "slab"))
    piece_rows = grad_rows.shape[0]
    position = lax.axis_index(("grp", "slab"))
    own_rows = lax.dynamic_slice_in_dim(spectral, position * piece_rows, piece_rows, 0)
    momentum_new = decay_rate * momentum + grad_rows
    updated_rows = own_rows - learn_rate * momentum_new
    spectral_new = lax.all_gather(updated_rows, ("grp", "slab"), axis=0, tiled=True)
    dense_new = dense - dense_rate * grad_dense
    return (field_now, trainer_loss, spectral_new, dense_new, momentum_new)


def solution(mesh):
    placed = (
        P("grp", "slab", None),
        P("grp", "slab", None),
        P("grp", "slab", None),
        P(("grp", "slab")),
        P(("grp", "slab")),
        P(("grp", "slab"), None),
        P(),
        P(),
        P(("grp", "slab"), None),
    )
    return jax.shard_map(
        local,
        mesh=mesh,
        in_specs=placed,
        out_specs=(P("grp", "slab", None), P("grp", "slab"), P(), P(), P(("grp", "slab"), None)),
        check_vma=False,
    )
```

profile of v0, /device:TPU:0, one launch (start us, length us, event | category | flops | bytes accessed | tf_op | source)
XLA Modules:
  0.0 314.7 jit_solution(17592519083051629129)
XLA Ops:
  9.3 4.9 %collective-permute-start.1 = (f32[1,8,512]{2,1,0:T(8,128)S(1)}, f32[1,8,512]{2,1,0:T(8,128)S(1)}, u32[]{:S(2)}, u32[]{:S(2)}) collective-permute-start(f32[1,8,512]{2,1,0:T(8,128)S(1)} %get-tuple-element.86), channel_id=1, source_target_pairs={{0,16},{1,17},{2,18},{3,19},{4,20},{5,21},{6,22},{7,23},{8,24},{9,... | collective-permute-start | bytes 49160 | tf_op jit(solution)/shard_map/ppermute | solution.py:22
  19.0 3.0 collective-permute-start.3
  24.0 2.3 collective-permute-start.5
  27.6 4.2 %collective-permute-done.4 = f32[1,8,512]{2,1,0:T(8,128)S(1)} collective-permute-done((f32[1,8,512]{2,1,0:T(8,128)S(1)}, f32[1,8,512]{2,1,0:T(8,128)S(1)}, u32[]{:S(2)}, u32[]{:S(2)}) %collective-permute-start.4) | collective-permute-done | bytes 16416 | tf_op jit(solution)/shard_map/ppermute | solution.py:24
  33.2 3.3 %collective-permute-start.7 = (f32[10,1,512]{2,1,0:T(1,128)S(1)}, f32[10,1,512]{2,1,0:T(1,128)S(1)}, u32[]{:S(2)}, u32[]{:S(2)}) collective-permute-start(f32[10,1,512]{2,1,0:T(1,128)S(1)} %get-tuple-element.72), channel_id=1, source_target_pairs={{0,1},{1,2},{2,3},{3,4},{4,5},{5,6},{6,7},{7,8},{8,9},{9,10},{10,1... | collective-permute-start | bytes 61448 | tf_op jit(solution)/shard_map/ppermute | solution.py:22
  38.8 32.3 %while.2 = (s32[]{:T(128)}, f32[16,512]{1,0:T(8,128)S(1)}, s32[16,2]{0,1:T(2,128)S(1)}, f32[16,128]{1,0:T(8,128)S(1)}, s32[]{:T(128)}, /*index=5*/s32[]{:T(128)}) while((s32[]{:T(128)}, f32[16,512]{1,0:T(8,128)S(1)}, s32[16,2]{0,1:T(2,128)S(1)}, f32[16,128]{1,0:T(8,128)S(1)}, s32[]{:T(128)}, /*index=5*/s32[]{:T(128)}) %tuple.61), condition=%wide.while_cond, body=%wide.while_body.sunk | while | flops 2 | bytes 2169 | solution.py:99
  71.1 1.4 convolution_negate_fusion
  72.5 1.4 fusion.38
  74.7 32.1 %while.3 = (s32[]{:T(128)}, f32[16,512]{1,0:T(8,128)S(1)}, s32[16,2]{0,1:T(2,128)S(1)}, f32[16,128]{1,0:T(8,128)S(1)}, s32[]{:T(128)}, /*index=5*/s32[]{:T(128)}) while((s32[]{:T(128)}, f32[16,512]{1,0:T(8,128)S(1)}, s32[16,2]{0,1:T(2,128)S(1)}, f32[16,128]{1,0:T(8,128)S(1)}, s32[]{:T(128)}, /*index=5*/s32[]{:T(128)}) %tuple.69), condition=%wide.while_cond.1, body=%wide.while_body.1.sunk | while | flops 2 | bytes 2169 | solution.py:99
  75.3 1.4 dynamic-slice.17
  77.3 1.4 dynamic-slice.17
  79.3 1.4 dynamic-slice.17
  81.2 1.4 dynamic-slice.17
  83.2 1.4 dynamic-slice.17
  85.2 1.4 dynamic-slice.17
  87.2 1.4 dynamic-slice.17
  95.2 1.4 dynamic-slice.17
  103.2 1.4 dynamic-slice.17
  105.2 1.4 dynamic-slice.17
  126.2 35.7 %all-reduce.7 = f32[16]{0:T(128)S(1)} all-reduce(f32[16]{0:T(128)S(1)} %fusion.11), channel_id=2, replica_groups=mesh['grp'=2,'slab'=16] {'slab'}, use_global_device_ids=true, to_apply=%region_1.3.clone | all-reduce | flops 16 | bytes 128
  167.0 37.0 %psum.7 = f32[68,64]{0,1:T(8,128)S(1)} all-reduce(f32[68,64]{0,1:T(8,128)S(1)} %pad_add_fusion.1), channel_id=1, replica_groups=mesh['grp'=2,'slab'=16] {'grp','slab'}, use_global_device_ids=true, to_apply=%region_6.8 | all-reduce | flops 4352 | bytes 34816 | tf_op jit(solution)/shard_map/psum | solution.py:121
  204.6 61.4 %reduce-scatter.2.cloned.1.call-done = f32[64,64]{1,0:T(8,128)} async-done(((f32[2048,64]{1,0:T(8,128)}), f32[64,64]{1,0:T(8,128)}) %reduce-scatter.2.cloned.1.call-update) | async-done | bytes 16400 | tf_op jit(solution)/shard_map/reduce_scatter | solution.py:120
  266.1 1.4 multiply_subtract_fusion.1
  267.5 39.3 %all_gather.3 = f32[2048,64]{1,0:T(8,128)S(1)} all-gather(f32[64,64]{1,0:T(8,128)S(1)} %get-tuple-element.61), channel_id=1, replica_groups=mesh['grp'=2,'slab'=16] {'grp','slab'}, dimensions={0}, use_global_device_ids=true | all-gather | bytes 540672 | tf_op jit(solution)/shard_map/all_gather | solution.py:127
  (216 shorter events, 90.9 us)
Async XLA Ops:
  7.2 9.2 %copy-start = (f32[8,8,512]{2,1,0:T(8,128)S(1)}, f32[8,8,512]{2,1,0:T(8,128)}, u32[]{:S(2)}) copy-start(f32[8,8,512]{2,1,0:T(8,128)} %param.11) | copy-start | bytes 393220
  7.2 10.2 %copy-start.2 = (f32[2048,64]{0,1:T(8,128)S(1)}, f32[2048,64]{0,1:T(8,128)}, u32[]{:S(2)}) copy-start(f32[2048,64]{0,1:T(8,128)} %param.17) | copy-start | bytes 1572868
  7.2 258.9 %reduce-scatter.2.cloned.1.call-start = ((), (), s32[]{:S(2)}) async-start(), calls=%async_computation.1 | async-start | bytes 1081344 | tf_op jit(solution)/shard_map/reduce_scatter | solution.py:120
  8.0 9.6 %collective-permute-start = (f32[1,8,512]{2,1,0:T(8,128)S(1)}, f32[1,8,512]{2,1,0:T(8,128)S(1)}, u32[]{:S(2)}, u32[]{:S(2)}) collective-permute-start(f32[1,8,512]{2,1,0:T(8,128)S(1)} %get-tuple-element.85), channel_id=1, source_target_pairs={{16,0},{17,1},{18,2},{19,3},{20,4},{21,5},{22,6},{23,7},{24,8},{25... | collective-permute-start | bytes 49160 | tf_op jit(solution)/shard_map/ppermute | solution.py:24
  9.3 8.3 %collective-permute-start.1 = (f32[1,8,512]{2,1,0:T(8,128)S(1)}, f32[1,8,512]{2,1,0:T(8,128)S(1)}, u32[]{:S(2)}, u32[]{:S(2)}) collective-permute-start(f32[1,8,512]{2,1,0:T(8,128)S(1)} %get-tuple-element.86), channel_id=1, source_target_pairs={{0,16},{1,17},{2,18},{3,19},{4,20},{5,21},{6,22},{7,23},{8,24},{9,... | collective-permute-start | bytes 49160 | tf_op jit(solution)/shard_map/ppermute | solution.py:22
  16.4 0.8 copy-start.1
  16.5 0.7 copy-start.6
  17.7 6.1 %collective-permute-start.2 = (f32[10,1,512]{2,1,0:T(1,128)S(1)}, f32[10,1,512]{2,1,0:T(1,128)S(1)}, u32[]{:S(2)}, u32[]{:S(2)}) collective-permute-start(f32[10,1,512]{2,1,0:T(1,128)S(1)} %get-tuple-element.73), channel_id=1, source_target_pairs={{1,0},{2,1},{3,2},{4,3},{5,4},{6,5},{7,6},{8,7},{9,8},{10,9},{11,1... | collective-permute-start | bytes 61448 | tf_op jit(solution)/shard_map/ppermute | solution.py:24
  19.0 4.8 %collective-permute-start.3 = (f32[10,1,512]{2,1,0:T(1,128)S(1)}, f32[10,1,512]{2,1,0:T(1,128)S(1)}, u32[]{:S(2)}, u32[]{:S(2)}) collective-permute-start(f32[10,1,512]{2,1,0:T(1,128)S(1)} %get-tuple-element.74), channel_id=1, source_target_pairs={{0,1},{1,2},{2,3},{3,4},{4,5},{5,6},{6,7},{7,8},{8,9},{9,10},{10,1... | collective-permute-start | bytes 61448 | tf_op jit(solution)/shard_map/ppermute | solution.py:22
  22.3 1.5 copy-start.3
  22.3 1.5 copy-start.4
  22.5 0.7 copy-start.8
  24.0 3.7 %collective-permute-start.5 = (f32[1,8,512]{2,1,0:T(8,128)S(1)}, f32[1,8,512]{2,1,0:T(8,128)S(1)}, u32[]{:S(2)}, u32[]{:S(2)}) collective-permute-start(f32[1,8,512]{2,1,0:T(8,128)S(1)} %get-tuple-element.75), channel_id=1, source_target_pairs={{0,16},{1,17},{2,18},{3,19},{4,20},{5,21},{6,22},{7,23},{8,24},{9,... | collective-permute-start | bytes 49160 | tf_op jit(solution)/shard_map/ppermute | solution.py:22
  26.2 5.6 %collective-permute-start.4 = (f32[1,8,512]{2,1,0:T(8,128)S(1)}, f32[1,8,512]{2,1,0:T(8,128)S(1)}, u32[]{:S(2)}, u32[]{:S(2)}) collective-permute-start(f32[1,8,512]{2,1,0:T(8,128)S(1)} %get-tuple-element.76), channel_id=1, source_target_pairs={{16,0},{17,1},{18,2},{19,3},{20,4},{21,5},{22,6},{23,7},{24,8},{25... | collective-permute-start | bytes 49160 | tf_op jit(solution)/shard_map/ppermute | solution.py:24
  31.9 5.3 %collective-permute-start.6 = (f32[10,1,512]{2,1,0:T(1,128)S(1)}, f32[10,1,512]{2,1,0:T(1,128)S(1)}, u32[]{:S(2)}, u32[]{:S(2)}) collective-permute-start(f32[10,1,512]{2,1,0:T(1,128)S(1)} %get-tuple-element.71), channel_id=1, source_target_pairs={{1,0},{2,1},{3,2},{4,3},{5,4},{6,5},{7,6},{8,7},{9,8},{10,9},{11,1... | collective-permute-start | bytes 61448 | tf_op jit(solution)/shard_map/ppermute | solution.py:24
  33.2 4.2 %collective-permute-start.7 = (f32[10,1,512]{2,1,0:T(1,128)S(1)}, f32[10,1,512]{2,1,0:T(1,128)S(1)}, u32[]{:S(2)}, u32[]{:S(2)}) collective-permute-start(f32[10,1,512]{2,1,0:T(1,128)S(1)} %get-tuple-element.72), channel_id=1, source_target_pairs={{0,1},{1,2},{2,3},{3,4},{4,5},{5,6},{6,7},{7,8},{8,9},{9,10},{10,1... | collective-permute-start | bytes 61448 | tf_op jit(solution)/shard_map/ppermute | solution.py:22
  124.5 0.7 copy-start.7
  204.0 62.1 %copy-start.5 = (f32[64,64]{1,0:T(8,128)S(1)}, f32[64,64]{1,0:T(8,128)}, u32[]{:S(2)}) copy-start(f32[64,64]{1,0:T(8,128)} %param.19) | copy-start | bytes 49156
Sparse Core Ops, SparseCore 0:
  124.6 141.4 reduce-scatter.1
where the time goes:
time: 316 us; the launch traced here: 315 us
  blocking collectives  112 us (35%)
  local copies, waits for them, and re-layouts  73.2 us (23%)
  waiting for transfers between devices  65.9 us (21%)
  matrix products  23.5 us (7%)
  starting transfers between devices  18.7 us (6%)
  between operations  14.5 us (5%)
  other arithmetic  6.66 us (2%)
    gather x128, local copies, waits for them, and re-layouts  64.1 us
    reduce_scatter x1, waiting for transfers between devices, local(): lax.psum_scatter(grad_spec, ('grp', 'slab'), scatter_dimension=0, tiled=T...  61.4 us
    all_gather x1, blocking collectives, local(): lax.all_gather(updated_rows, ('grp', 'slab'), axis=0, tiled=True)  39.3 us
    psum x1, blocking collectives, local(): grad_dense = lax.psum(grad_dense, ('grp', 'slab'))  37 us
    unnamed x1, blocking collectives  35.7 us
    ppermute x4, starting transfers between devices, extended(): lax.ppermute(tail, axis, [(i, (i + 1) % count) for i in range(ends)])  13.5 us
  transfers between devices with their start and end apart: 9, of which 3 were waited for; matrix products, arithmetic and copies ran while one was open for 4% of the time, Pallas kernels for 0%

commit v1 on v0

--- a/solution.py
+++ b/solution.py
@@ -9,6 +9,11 @@
 decay_rate = 0.9
 learn_rate = 0.5
 dense_rate = 3.0
+
+
+def feed_signs(t0, axis_key):
+    carry_in = lax.all_gather(t0, axis_name=axis_key).sum(axis=0)
+    return carry_in
 
 
 def extended(cells, sides, width):
@@ -118,7 +123,7 @@
         1, 1
     )
     grad_rows = lax.psum_scatter(grad_spec, ("grp", "slab"), scatter_dimension=0, tiled=True)
-    grad_dense = lax.psum(grad_dense, ("grp", "slab"))
+    grad_dense = feed_signs(grad_dense, ("grp", "slab"))
     piece_rows = grad_rows.shape[0]
     position = lax.axis_index(("grp", "slab"))
     own_rows = lax.dynamic_slice_in_dim(spectral, position * piece_rows, piece_rows, 0)

time: 316 us -> 349 us (1.10)
  waiting for transfers between devices: 65.9 us -> 91.9 us
  matrix products: 23.5 us -> 27.7 us
    all_gather x0 -> x1, blocking collectives: none -> 39.7 us  [feed_signs(): carry_in = lax.all_gather(t0, axis_name=axis_key).sum(axis=0)]
    psum x1 -> x0, blocking collectives: 37 us -> none  [local(): grad_dense = lax.psum(grad_dense, ('grp', 'slab'))]
    reduce_scatter x1, waiting for transfers between devices: 61.4 us -> 87.5 us  [local(): lax.psum_scatter(grad_spec, ('grp', 'slab'), scatter_dimension=0, tiled=T...]
  transfers between devices with their start and end apart: 9 -> 9, of which waited for: 3 -> 3; matrix products, arithmetic and copies ran while one was open for 4% -> 3% of each run, Pallas kernels for 0% -> 0%
where the time goes in v1:
time: 349 us; the launch traced here: 348 us
  blocking collectives  115 us (33%)
  waiting for transfers between devices  91.9 us (26%)
  local copies, waits for them, and re-layouts  73.1 us (21%)
  matrix products  27.7 us (8%)
  starting transfers between devices  18.7 us (5%)
  between operations  14.5 us (4%)
  other arithmetic  6.79 us (2%)
    reduce_scatter x1, waiting for transfers between devices, local(): lax.psum_scatter(grad_spec, ('grp', 'slab'), scatter_dimension=0, tiled=T...  87.5 us
    gather x128, local copies, waits for them, and re-layouts  63.9 us
    all_gather x1, blocking collectives, feed_signs(): carry_in = lax.all_gather(t0, axis_name=axis_key).sum(axis=0)  39.7 us
    all_gather x1, blocking collectives, local(): lax.all_gather(updated_rows, ('grp', 'slab'), axis=0, tiled=True)  39.3 us
    unnamed x1, blocking collectives  35.6 us
    ppermute x4, starting transfers between devices, extended(): lax.ppermute(tail, axis, [(i, (i + 1) % count) for i in range(ends)])  13.5 us
  transfers between devices with their start and end apart: 9, of which 3 were waited for; matrix products, arithmetic and copies ran while one was open for 3% of the time, Pallas kernels for 0%

profile of v1, /device:TPU:0, one launch (start us, length us, event | category | flops | bytes accessed | tf_op | source)
XLA Modules:
  0.0 347.6 jit_solution(13756954468196533733)
XLA Ops:
  9.3 4.9 %collective-permute-start.1 = (f32[1,8,512]{2,1,0:T(8,128)S(1)}, f32[1,8,512]{2,1,0:T(8,128)S(1)}, u32[]{:S(2)}, u32[]{:S(2)}) collective-permute-start(f32[1,8,512]{2,1,0:T(8,128)S(1)} %get-tuple-element.86), channel_id=1, source_target_pairs={{0,16},{1,17},{2,18},{3,19},{4,20},{5,21},{6,22},{7,23},{8,24},{9,... | collective-permute-start | bytes 49160 | tf_op jit(solution)/shard_map/ppermute | solution.py:27
  19.0 3.0 collective-permute-start.3
  24.0 2.3 collective-permute-start.5
  27.6 4.2 %collective-permute-done.4 = f32[1,8,512]{2,1,0:T(8,128)S(1)} collective-permute-done((f32[1,8,512]{2,1,0:T(8,128)S(1)}, f32[1,8,512]{2,1,0:T(8,128)S(1)}, u32[]{:S(2)}, u32[]{:S(2)}) %collective-permute-start.4) | collective-permute-done | bytes 16416 | tf_op jit(solution)/shard_map/ppermute | solution.py:29
  33.2 3.3 collective-permute-start.7
  38.8 32.1 %while.2 = (s32[]{:T(128)}, f32[16,512]{1,0:T(8,128)S(1)}, s32[16,2]{0,1:T(2,128)S(1)}, f32[16,128]{1,0:T(8,128)S(1)}, s32[]{:T(128)}, /*index=5*/s32[]{:T(128)}) while((s32[]{:T(128)}, f32[16,512]{1,0:T(8,128)S(1)}, s32[16,2]{0,1:T(2,128)S(1)}, f32[16,128]{1,0:T(8,128)S(1)}, s32[]{:T(128)}, /*index=5*/s32[]{:T(128)}) %tuple.61), condition=%wide.while_cond, body=%wide.while_body.sunk | while | flops 2 | bytes 2169 | solution.py:104
  70.9 1.4 convolution_negate_fusion
  72.3 1.4 fusion.38
  74.4 32.1 %while.3 = (s32[]{:T(128)}, f32[16,512]{1,0:T(8,128)S(1)}, s32[16,2]{0,1:T(2,128)S(1)}, f32[16,128]{1,0:T(8,128)S(1)}, s32[]{:T(128)}, /*index=5*/s32[]{:T(128)}) while((s32[]{:T(128)}, f32[16,512]{1,0:T(8,128)S(1)}, s32[16,2]{0,1:T(2,128)S(1)}, f32[16,128]{1,0:T(8,128)S(1)}, s32[]{:T(128)}, /*index=5*/s32[]{:T(128)}) %tuple.69), condition=%wide.while_cond.1, body=%wide.while_body.1.sunk | while | flops 2 | bytes 2169 | solution.py:104
  75.1 1.4 dynamic-slice.17
  77.0 1.4 dynamic-slice.17
  85.0 1.4 dynamic-slice.17
  87.0 1.4 dynamic-slice.17
  95.0 1.4 dynamic-slice.17
  113.5 2.1 fusion.186
  115.6 1.6 fusion.80
  117.2 1.6 fusion.78
  121.1 1.8 fusion.84
  122.9 35.6 %all-reduce.7 = f32[16]{0:T(128)S(1)} all-reduce(f32[16]{0:T(128)S(1)} %fusion.11), channel_id=3, replica_groups=mesh['grp'=2,'slab'=16] {'slab'}, use_global_device_ids=true, to_apply=%region_1.3.clone | all-reduce | flops 16 | bytes 128
  159.3 2.6 fusion.2
  171.1 39.7 %all-gather.1 = f32[32,68,64]{1,2,0:T(8,128)S(1)} all-gather(f32[1,68,64]{1,2,0:T(8,128)S(1)} %add_bitcast_fusion), channel_id=2, replica_groups=mesh['grp'=2,'slab'=16] {'grp','slab'}, dimensions={0}, use_global_device_ids=true | all-gather | bytes 574464 | tf_op jit(solution)/shard_map/all_gather | solution.py:15
  211.5 87.5 %reduce-scatter.2.cloned.1.call-done = f32[64,64]{1,0:T(8,128)} async-done(((f32[2048,64]{1,0:T(8,128)}), f32[64,64]{1,0:T(8,128)}) %reduce-scatter.2.cloned.1.call-update) | async-done | bytes 16400 | tf_op jit(solution)/shard_map/reduce_scatter | solution.py:125
  299.0 1.4 multiply_subtract_fusion.1
  300.3 39.3 %all_gather.9 = f32[2048,64]{1,0:T(8,128)S(1)} all-gather(f32[64,64]{1,0:T(8,128)S(1)} %get-tuple-element.61), channel_id=1, replica_groups=mesh['grp'=2,'slab'=16] {'grp','slab'}, dimensions={0}, use_global_device_ids=true | all-gather | bytes 540672 | tf_op jit(solution)/shard_map/all_gather | solution.py:132
  (227 shorter events, 92.3 us)
Async XLA Ops:
  7.2 9.2 %copy-start = (f32[8,8,512]{2,1,0:T(8,128)S(1)}, f32[8,8,512]{2,1,0:T(8,128)}, u32[]{:S(2)}) copy-start(f32[8,8,512]{2,1,0:T(8,128)} %param.11) | copy-start | bytes 393220
  7.2 10.2 %copy-start.5 = (f32[2048,64]{0,1:T(8,128)S(1)}, f32[2048,64]{0,1:T(8,128)}, u32[]{:S(2)}) copy-start(f32[2048,64]{0,1:T(8,128)} %param.17) | copy-start | bytes 1572868
  7.2 291.8 %reduce-scatter.2.cloned.1.call-start = ((), (), s32[]{:S(2)}) async-start(), calls=%async_computation.1 | async-start | bytes 1081344 | tf_op jit(solution)/shard_map/reduce_scatter | solution.py:125
  8.0 9.6 %collective-permute-start = (f32[1,8,512]{2,1,0:T(8,128)S(1)}, f32[1,8,512]{2,1,0:T(8,128)S(1)}, u32[]{:S(2)}, u32[]{:S(2)}) collective-permute-start(f32[1,8,512]{2,1,0:T(8,128)S(1)} %get-tuple-element.85), channel_id=1, source_target_pairs={{16,0},{17,1},{18,2},{19,3},{20,4},{21,5},{22,6},{23,7},{24,8},{25... | collective-permute-start | bytes 49160 | tf_op jit(solution)/shard_map/ppermute | solution.py:29
  9.3 8.3 %collective-permute-start.1 = (f32[1,8,512]{2,1,0:T(8,128)S(1)}, f32[1,8,512]{2,1,0:T(8,128)S(1)}, u32[]{:S(2)}, u32[]{:S(2)}) collective-permute-start(f32[1,8,512]{2,1,0:T(8,128)S(1)} %get-tuple-element.86), channel_id=1, source_target_pairs={{0,16},{1,17},{2,18},{3,19},{4,20},{5,21},{6,22},{7,23},{8,24},{9,... | collective-permute-start | bytes 49160 | tf_op jit(solution)/shard_map/ppermute | solution.py:27
  16.4 0.8 copy-start.2
  16.5 0.7 copy-start.11
  17.7 6.1 %collective-permute-start.2 = (f32[10,1,512]{2,1,0:T(1,128)S(1)}, f32[10,1,512]{2,1,0:T(1,128)S(1)}, u32[]{:S(2)}, u32[]{:S(2)}) collective-permute-start(f32[10,1,512]{2,1,0:T(1,128)S(1)} %get-tuple-element.73), channel_id=1, source_target_pairs={{1,0},{2,1},{3,2},{4,3},{5,4},{6,5},{7,6},{8,7},{9,8},{10,9},{11,1... | collective-permute-start | bytes 61448 | tf_op jit(solution)/shard_map/ppermute | solution.py:29
  19.0 4.8 %collective-permute-start.3 = (f32[10,1,512]{2,1,0:T(1,128)S(1)}, f32[10,1,512]{2,1,0:T(1,128)S(1)}, u32[]{:S(2)}, u32[]{:S(2)}) collective-permute-start(f32[10,1,512]{2,1,0:T(1,128)S(1)} %get-tuple-element.74), channel_id=1, source_target_pairs={{0,1},{1,2},{2,3},{3,4},{4,5},{5,6},{6,7},{7,8},{8,9},{9,10},{10,1... | collective-permute-start | bytes 61448 | tf_op jit(solution)/shard_map/ppermute | solution.py:27
  22.3 1.5 copy-start.8
  22.3 1.5 copy-start.9
  22.5 0.7 copy-start.13
  24.0 3.7 %collective-permute-start.5 = (f32[1,8,512]{2,1,0:T(8,128)S(1)}, f32[1,8,512]{2,1,0:T(8,128)S(1)}, u32[]{:S(2)}, u32[]{:S(2)}) collective-permute-start(f32[1,8,512]{2,1,0:T(8,128)S(1)} %get-tuple-element.75), channel_id=1, source_target_pairs={{0,16},{1,17},{2,18},{3,19},{4,20},{5,21},{6,22},{7,23},{8,24},{9,... | collective-permute-start | bytes 49160 | tf_op jit(solution)/shard_map/ppermute | solution.py:27
  26.2 5.6 %collective-permute-start.4 = (f32[1,8,512]{2,1,0:T(8,128)S(1)}, f32[1,8,512]{2,1,0:T(8,128)S(1)}, u32[]{:S(2)}, u32[]{:S(2)}) collective-permute-start(f32[1,8,512]{2,1,0:T(8,128)S(1)} %get-tuple-element.76), channel_id=1, source_target_pairs={{16,0},{17,1},{18,2},{19,3},{20,4},{21,5},{22,6},{23,7},{24,8},{25... | collective-permute-start | bytes 49160 | tf_op jit(solution)/shard_map/ppermute | solution.py:29
  31.9 5.3 %collective-permute-start.6 = (f32[10,1,512]{2,1,0:T(1,128)S(1)}, f32[10,1,512]{2,1,0:T(1,128)S(1)}, u32[]{:S(2)}, u32[]{:S(2)}) collective-permute-start(f32[10,1,512]{2,1,0:T(1,128)S(1)} %get-tuple-element.71), channel_id=1, source_target_pairs={{1,0},{2,1},{3,2},{4,3},{5,4},{6,5},{7,6},{8,7},{9,8},{10,9},{11,1... | collective-permute-start | bytes 61448 | tf_op jit(solution)/shard_map/ppermute | solution.py:29
  33.2 4.2 %collective-permute-start.7 = (f32[10,1,512]{2,1,0:T(1,128)S(1)}, f32[10,1,512]{2,1,0:T(1,128)S(1)}, u32[]{:S(2)}, u32[]{:S(2)}) collective-permute-start(f32[10,1,512]{2,1,0:T(1,128)S(1)} %get-tuple-element.72), channel_id=1, source_target_pairs={{0,1},{1,2},{2,3},{3,4},{4,5},{5,6},{6,7},{7,8},{8,9},{9,10},{10,1... | collective-permute-start | bytes 61448 | tf_op jit(solution)/shard_map/ppermute | solution.py:27
  120.2 0.7 copy-start.12
  159.3 2.6 copy-start.4
  161.9 1.0 copy-start.3
  161.9 1.0 copy-start.7
  162.9 1.0 copy-start.1
  166.1 1.0 copy-start.6
  210.9 88.1 %copy-start.10 = (f32[64,64]{1,0:T(8,128)S(1)}, f32[64,64]{1,0:T(8,128)}, u32[]{:S(2)}) copy-start(f32[64,64]{1,0:T(8,128)} %param.19) | copy-start | bytes 49156
Sparse Core Ops, SparseCore 0:
  166.2 132.7 reduce-scatter.1
